TPU v7x, 32 devices: a whole 2x2x4 slice. The times are simulated.
32 devices in a mesh: rows: 16 (over z, y, x), rep: 2 (over core).
Axes of the slice: x: 2, y: 2, z: 4, core: 2. Of those that a mesh axis runs over, the one named last changes fastest.
Arguments:
- features: bfloat16 [4096, 128], P(('rows', 'rep')), may hold values from -6 to 6
- tile_counts: int32 [4096, 128, 128], P(('rows', 'rep')), may hold values from 0 to 3, as said below
- tile_row: int32 [4096], P(('rows', 'rep')), may hold values from 0 to 1
- tile_col: int32 [4096], P(('rows', 'rep')), may hold values from 0 to 31, as said below
- label_ids: int32 [2048], P(('rows', 'rep')), may hold values from 0 to 4095, as said below
- cotangent: bfloat16 [4096, 256], P(('rows', 'rep')), may hold values from -6 to 6
- self_weight: bfloat16 [128, 256], replicated, may hold values from -0.5 to 0.5
- neigh_weight: bfloat16 [128, 256], replicated, may hold values from -0.5 to 0.5
Outputs:
- activation: bfloat16 [4096, 256], P(('rows', 'rep'))
- grad_features: float32 [4096, 128], P(('rows', 'rep'))
- grad_self: float32 [128, 256], replicated
- grad_neigh: float32 [128, 256], replicated
Inputs may be any that keep to these rules, and one draw needn't show every extreme that they name: `tile_counts`: edge counts of one tile; most entries are zero. `tile_col`: every tile held by a device of rep index c names a column block of the feature rows of some device of rep index c. On each device, at most 16 tiles name column blocks held by devices of one rows index, and exactly 16 do for some rows index. `label_ids`: the ids of one device's 64 labels are distinct and lie among that device's own feature rows.
All inputs are finite; a program needn't handle non-finite values.
Results may differ from a plain program's by a relative error of at most 0.0053.
Values may be sent and summed in bfloat16 or wider, within the bound.
A program may use at most 128 MiB of HBM per device.

v0:
```python
import jax
import jax.numpy as jnp
from jax import lax
from jax.sharding import PartitionSpec as P

edge_moment = 14.0 / 96.0


def derivative(preact, masked):
    sigma = jax.nn.sigmoid(preact)
    return (masked.astype(jnp.float32) * sigma * (1.0 + preact * (1.0 - sigma))).astype(
        jnp.bfloat16
    )


def shards(
    features, tile_counts, tile_row, tile_col, label_ids, cotangent, self_weight, neigh_weight
):
    half_rows, width_in = features.shape
    block_size = tile_counts.shape[1]
    tile_total = tile_counts.shape[0]
    rep_count = lax.axis_size("rep")
    row_count = lax.axis_size("rows")
    per_half = half_rows // block_size
    row_blocks = rep_count * per_half
    scale = (edge_moment * tile_total * rep_count * block_size / row_blocks) ** (-0.5)
    gathered = lax.all_gather(features, "rows", axis=0, tiled=True)
    local_col = tile_col // (rep_count * per_half) * per_half + tile_col % per_half
    panels = gathered.reshape(-1, block_size, width_in)[local_col]
    counts = tile_counts.astype(jnp.bfloat16)
    products = jnp.einsum("tij,tjf->tif", counts, panels, preferred_element_type=jnp.float32)
    owner_table = (tile_row[:, None] == jnp.arange(row_blocks, dtype=jnp.int32)[None, :]).astype(
        jnp.float32
    )
    partial_rows = jnp.einsum(
        "tr,tif->rif", owner_table, products, precision=lax.Precision.HIGHEST
    ).reshape(row_blocks * block_size, width_in)
    local_ids = label_ids % half_rows
    label_mask = jnp.any(
        local_ids[:, None] == jnp.arange(half_rows, dtype=jnp.int32)[None, :], axis=0
    )
    masked = cotangent * label_mask[:, None].astype(jnp.bfloat16)
    rep_place = lax.axis_index("rep")
    neighbour_sum = lax.psum(partial_rows, "rep") * scale
    group_feat, group_masked = (
        lax.all_gather(features, "rep", axis=0, tiled=True),
        lax.all_gather(masked, "rep", axis=0, tiled=True),
    )
    neighbour = neighbour_sum.astype(jnp.bfloat16)
    preact = jnp.dot(group_feat, self_weight, preferred_element_type=jnp.float32) + jnp.dot(
        neighbour, neigh_weight, preferred_element_type=jnp.float32
    )
    activation_all = jax.nn.silu(preact).astype(jnp.bfloat16)
    delta_all = derivative(preact, group_masked)
    back = jnp.einsum(
        "nh,fh->nf", delta_all, neigh_weight, preferred_element_type=jnp.float32
    ).astype(jnp.bfloat16)
    activation = lax.dynamic_slice_in_dim(activation_all, rep_place * half_rows, half_rows, 0)
    delta_own = lax.dynamic_slice_in_dim(delta_all, rep_place * half_rows, half_rows, 0)
    neighbour_own = lax.dynamic_slice_in_dim(neighbour, rep_place * half_rows, half_rows, 0)
    self_part = jnp.einsum("nf,nh->fh", features, delta_own, preferred_element_type=jnp.float32)
    neigh_part = jnp.einsum(
        "nf,nh->fh", neighbour_own, delta_own, preferred_element_type=jnp.float32
    )
    pair_self, pair_neigh = lax.psum((self_part, neigh_part), "rep")
    self_total, neigh_total = lax.psum((pair_self, pair_neigh), "rows")
    grad_scale = float(label_ids.shape[0] * row_count * rep_count) ** (-0.5)
    picked = back.reshape(row_blocks, block_size, width_in)[tile_row]
    col_terms = jnp.einsum(
        "tij,tif->tjf", counts, picked, preferred_element_type=jnp.float32
    ).astype(jnp.bfloat16)
    count = half_rows * lax.axis_size("rows")
    block_count = count // block_size
    placing = (local_col[None, :] == jnp.arange(block_count, dtype=jnp.int32)[:, None]).astype(
        jnp.bfloat16
    )
    summed = jnp.einsum("bt,tif->bif", placing, col_terms, preferred_element_type=jnp.float32)
    scattered = lax.psum_scatter(
        summed.reshape(count, width_in), "rows", scatter_dimension=0, tiled=True
    )
    own_term = jnp.einsum("nh,fh->nf", delta_own, self_weight, preferred_element_type=jnp.float32)
    grad_features = own_term + scale * scattered
    return (activation, grad_features, grad_scale * self_total, grad_scale * neigh_total)


def solution(mesh):
    placed = (
        P(("rows", "rep"), None),
        P(("rows", "rep"), None, None),
        P(("rows", "rep")),
        P(("rows", "rep")),
        P(("rows", "rep")),
        P(("rows", "rep"), None),
        P(),
        P(),
    )
    return jax.shard_map(
        shards,
        mesh=mesh,
        in_specs=placed,
        out_specs=(P(("rows", "rep"), None), P(("rows", "rep"), None), P(), P()),
        check_vma=False,
    )
```

profile of v0, /device:TPU:0, one launch (start us, length us, event | category | flops | bytes accessed | tf_op | source)
XLA Modules:
  0.0 322.9 jit_solution(7102248980317323099)
XLA Ops:
  7.2 0.7 compare_select_fusion.1
  7.9 45.6 %all_gather.10 = bf16[2048,128]{1,0:T(8,128)(2,1)S(1)} all-gather(bf16[128,128]{1,0:T(8,128)(2,1)} %param.8), channel_id=1, replica_groups=mesh['rows'=16,'rep'=2] {'rows'}, dimensions={0}, use_global_device_ids=true | all-gather | bytes 557056 | tf_op jit(solution)/shard_map/all_gather | solution.py:27
  53.5 3.1 gather_fusion
  56.5 11.0 %convolution_bitcast_fusion = f32[128,128,128]{1,2,0:T(8,128)} fusion(bf16[128,128,128]{2,1,0:T(8,128)(2,1)} %gather_fusion, s32[128,128,128]{2,1,0:T(8,128)} %param.9), kind=kOutput, calls=%fused_computation.3 | convolution fusion | flops 538968064 | bytes 20971520 | tf_op jit(solution)/shard_map/tij,tjf->tif/dot_general | solution.py:31
  67.5 9.3 %copy.29 = f32[128,128,128]{2,0,1:T(8,128)} copy(f32[128,128,128]{1,2,0:T(8,128)} %convolution_bitcast_fusion) | data formatting | bytes 16777216 | tf_op jit(solution)/shard_map/tij,tjf->tif/dot_general | solution.py:31
  76.8 6.2 %fusion.13 = f32[2,128,128]{2,0,1:T(2,128)S(1)} fusion(f32[128,128,128]{2,0,1:T(8,128)} %copy.29, s32[128]{0:T(128)S(1)} %copy-done.4), kind=kOutput, calls=%fused_computation.35 | convolution fusion | flops 50331904 | bytes 8520192 | tf_op jit(solution)/shard_map/tr,tif->rif/dot_general | solution.py:35
  83.8 1.9 all_gather.9
  86.0 1.9 all_gather.11
  87.9 9.7 %all-reduce.6.cloned.1.call-done = f32[256,128]{1,0:T(8,128)} async-done(((f32[256,128]{1,0:T(8,128)}), f32[256,128]{1,0:T(8,128)}) %all-reduce.6.cloned.1.call-update) | async-done | bytes 131088 | tf_op jit(solution)/shard_map/psum | solution.py:44
  97.6 0.9 multiply_convert_fusion.1
  98.8 0.9 fusion.3
  99.7 0.9 convolution_bitcast_fusion.1
  100.8 3.0 gather_fusion.1
  103.9 8.3 %convert_bitcast_fusion = bf16[128,128,128]{1,2,0:T(8,128)(2,1)} fusion(bf16[128,128,128]{2,1,0:T(8,128)(2,1)} %gather_fusion.1, s32[128,128,128]{2,1,0:T(8,128)} %param.9), kind=kOutput, calls=%fused_computation.2 | convolution fusion | flops 541065216 | bytes 16777216 | tf_op jit(solution)/shard_map/tij,tif->tjf/dot_general | solution.py:69
  112.2 6.7 %copy.32 = bf16[128,128,128]{2,0,1:T(8,128)(2,1)} copy(bf16[128,128,128]{1,2,0:T(8,128)(2,1)} %convert_bitcast_fusion) | data formatting | bytes 8388608 | tf_op jit(solution)/shard_map/convert_element_type | solution.py:71
  118.9 1.5 all-reduce.10.cloned.1.call-done
  120.5 2.8 fusion.10
  123.4 1.3 copy.33
  125.3 109.8 %all-reduce.8.cloned.1.call-done = (f32[128,256]{0,1:T(8,128)}, f32[128,256]{0,1:T(8,128)}) async-done(((f32[128,256]{0,1:T(8,128)}, f32[128,256]{0,1:T(8,128)}), (f32[128,256]{0,1:T(8,128)}, f32[128,256]{0,1:T(8,128)})) %all-reduce.8.cloned.1.call-update) | async-done | bytes 262160 | tf_op jit(solution)/shard_map/psum | solution.py:66
  235.1 1.0 broadcast_multiply_fusion
  236.1 0.8 copy.35
  236.9 0.8 copy.36
  237.6 77.1 %reduce-scatter.2.cloned.1.call-done = f32[128,128]{1,0:T(8,128)} async-done(((f32[2048,128]{1,0:T(8,128)}), f32[128,128]{1,0:T(8,128)}) %reduce-scatter.2.cloned.1.call-update) | async-done | bytes 65552 | tf_op jit(solution)/shard_map/reduce_scatter | solution.py:78
  314.8 1.6 convolution_add_fusion.1
  (32 shorter events, 2.4 us)
Async XLA Ops:
  7.2 91.4 %copy-start = (bf16[128,256]{1,0:T(8,128)(2,1)S(1)}, bf16[128,256]{1,0:T(8,128)(2,1)}, u32[]{:S(2)}) copy-start(bf16[128,256]{1,0:T(8,128)(2,1)} %param.15) | copy-start | bytes 196612
  7.2 90.5 %all-reduce.6.cloned.1.call-start = ((), (), s32[]{:S(2)}) async-start(), calls=%async_computation.1 | async-start | bytes 262144 | tf_op jit(solution)/shard_map/psum | solution.py:44
  67.5 9.3 %copy-start.4 = (s32[128]{0:T(128)S(1)}, s32[128]{0:T(128)}, u32[]{:S(2)}) copy-start(s32[128]{0:T(128)} %param.10) | copy-start | bytes 1540
  76.8 7.0 %copy-start.1 = (bf16[128,128]{1,0:T(8,128)(2,1)S(1)}, bf16[128,128]{1,0:T(8,128)(2,1)}, u32[]{:S(2)}) copy-start(bf16[128,128]{1,0:T(8,128)(2,1)} %param.8) | copy-start | bytes 98308
  76.8 8.9 %copy-start.5 = (s32[64]{0:T(128)S(1)}, s32[64]{0:T(128)}, u32[]{:S(2)}) copy-start(s32[64]{0:T(128)} %param.12) | copy-start | bytes 772
  76.8 9.0 %copy-start.2 = (bf16[128,256]{1,0:T(8,128)(2,1)S(1)}, bf16[128,256]{1,0:T(8,128)(2,1)}, u32[]{:S(2)}) copy-start(bf16[128,256]{1,0:T(8,128)(2,1)} %param.14) | copy-start | bytes 196612
  76.8 9.1 %copy-start.3 = (bf16[128,256]{1,0:T(8,128)(2,1)S(1)}, bf16[128,256]{1,0:T(8,128)(2,1)}, u32[]{:S(2)}) copy-start(bf16[128,256]{1,0:T(8,128)(2,1)} %param.13) | copy-start | bytes 196612
  83.7 36.7 %all-reduce.10.cloned.1.call-start = ((), (), s32[]{:S(2)}) async-start(), calls=%async_computation.4 | async-start | bytes 524288 | tf_op jit(solution)/shard_map/psum | solution.py:65
  100.8 134.3 %all-reduce.8.cloned.1.call-start = ((), (), s32[]{:S(2)}) async-start(), calls=%async_computation.3 | async-start | bytes 524288 | tf_op jit(solution)/shard_map/psum | solution.py:66
  120.5 194.3 %reduce-scatter.2.cloned.1.call-start = ((), (), s32[]{:S(2)}) async-start(), calls=%async_computation.2 | async-start | bytes 1114112 | tf_op jit(solution)/shard_map/reduce_scatter | solution.py:78
Sparse Core Ops, SparseCore 0:
  83.8 13.7 all-reduce.5
  100.9 19.4 all-reduce.9
  125.7 109.3 all-reduce.7
  237.2 77.4 reduce-scatter.1
where the time goes:
time: 323 us
  waiting for transfers between devices  198 us (61%)
  blocking collectives  49.3 us (15%)
  matrix products  32.3 us (10%)
  local copies, waits for them, and re-layouts  25.6 us (8%)
  between operations  13.9 us (4%)
  other arithmetic  3.44 us (1%)
    psum x1, waiting for transfers between devices, shards(): self_total, neigh_total = lax.psum((pair_self, pair_neigh), 'rows')  110 us
    reduce_scatter x1, waiting for transfers between devices, shards(): lax.psum_scatter(summed.reshape(count, width_in), 'rows', scatter_dimensi...  77.1 us
    all_gather x1, blocking collectives, shards(): gathered = lax.all_gather(features, 'rows', axis=0, tiled=True)  45.6 us
    dot_general x1, matrix products, shards(): jnp.einsum('tij,tjf->tif', counts, panels, preferred_element_type=jnp.flo...  11 us
    psum x1, waiting for transfers between devices, shards(): neighbour_sum = lax.psum(partial_rows, 'rep') * scale  9.71 us
    dot_general x1, local copies, waits for them, and re-layouts, shards(): jnp.einsum('tij,tjf->tif', counts, panels, preferred_element_type=jnp.flo...  9.29 us
    dot_general x1, matrix products, shards(): jnp.einsum('tij,tif->tjf', counts, picked, preferred_element_type=jnp.flo...  8.31 us
    convert_element_type x1, local copies, waits for them, and re-layouts, shards(): col_terms = jnp.einsum('tij,tif->tjf', counts, picked, preferred_element_...  6.75 us
  transfers between devices with their start and end apart: 4, of which 4 were waited for; matrix products, arithmetic and copies ran while one was open for 8% of the time, Pallas kernels for 0%

commit v1 on v0

--- a/solution.py
+++ b/solution.py
@@ -24,7 +24,9 @@
     per_half = half_rows // block_size
     row_blocks = rep_count * per_half
     scale = (edge_moment * tile_total * rep_count * block_size / row_blocks) ** (-0.5)
-    gathered = lax.all_gather(features, "rows", axis=0, tiled=True)
+    gathered = jnp.concatenate(
+        lax.all_to_all(jnp.stack([features] * lax.axis_size("rows")), "rows", 0, 0), axis=0
+    )
     local_col = tile_col // (rep_count * per_half) * per_half + tile_col % per_half
     panels = gathered.reshape(-1, block_size, width_in)[local_col]
     counts = tile_counts.astype(jnp.bfloat16)

time: 323 us -> 305 us (0.944)
  blocking collectives: 49.3 us -> 3.97 us
  waiting for transfers between devices: 198 us -> 212 us
  starting transfers between devices: 0.16 us -> 8.5 us
    all_gather x1 -> x0, blocking collectives: 45.6 us -> none  [shards(): gathered = lax.all_gather(features, 'rows', axis=0, tiled=True)]
    all_to_all x0 -> x1, waiting for transfers between devices: none -> 8.92 us  [shards(): lax.all_to_all(jnp.stack([features] * lax.axis_size('rows')), 'rows', 0, 0)]
    all_to_all x0 -> x1, starting transfers between devices: none -> 8.34 us  [shards(): lax.all_to_all(jnp.stack([features] * lax.axis_size('rows')), 'rows', 0, 0)]
    psum x1, waiting for transfers between devices: 9.71 us -> 14.4 us  [shards(): neighbour_sum = lax.psum(partial_rows, 'rep') * scale]
  transfers between devices with their start and end apart: 4 -> 5, of which waited for: 4 -> 5; matrix products, arithmetic and copies ran while one was open for 8% -> 10% of each run, Pallas kernels for 0% -> 0%
where the time goes in v1:
time: 305 us; the launch traced here: 304 us
  waiting for transfers between devices  212 us (70%)
  matrix products  33.1 us (11%)
  local copies, waits for them, and re-layouts  27.3 us (9%)
  between operations  13.9 us (5%)
  starting transfers between devices  8.5 us (3%)
  other arithmetic  5.58 us (2%)
  blocking collectives  3.97 us (1%)
    psum x1, waiting for transfers between devices, shards(): self_total, neigh_total = lax.psum((pair_self, pair_neigh), 'rows')  110 us
    reduce_scatter x1, waiting for transfers between devices, shards(): lax.psum_scatter(summed.reshape(count, width_in), 'rows', scatter_dimensi...  77.1 us
    psum x1, waiting for transfers between devices, shards(): neighbour_sum = lax.psum(partial_rows, 'rep') * scale  14.4 us
    dot_general x1, matrix products, shards(): jnp.einsum('tij,tjf->tif', counts, panels, preferred_element_type=jnp.flo...  11 us
    dot_general x1, local copies, waits for them, and re-layouts, shards(): jnp.einsum('tij,tjf->tif', counts, panels, preferred_element_type=jnp.flo...  9.29 us
    all_to_all x1, waiting for transfers between devices, shards(): lax.all_to_all(jnp.stack([features] * lax.axis_size('rows')), 'rows', 0, 0)  8.92 us
    all_to_all x1, starting transfers between devices, shards(): lax.all_to_all(jnp.stack([features] * lax.axis_size('rows')), 'rows', 0, 0)  8.34 us
    dot_general x1, matrix products, shards(): jnp.einsum('tij,tif->tjf', counts, picked, preferred_element_type=jnp.flo...  8.31 us
  transfers between devices with their start and end apart: 5, of which 5 were waited for; matrix products, arithmetic and copies ran while one was open for 10% of the time, Pallas kernels for 0%

profile of v1, /device:TPU:0, one launch (start us, length us, event | category | flops | bytes accessed | tf_op | source)
XLA Modules:
  0.0 304.2 jit_solution(18413748958146388931)
XLA Ops:
  7.2 1.7 stack.2
  8.9 8.3 %all-to-all-start = ((bf16[16,128,128]{2,1,0:T(8,128)(2,1)}), bf16[16,128,128]{2,1,0:T(8,128)(2,1)S(1)}, u32[]{:S(2)}, u32[]{:S(2)}) async-start(bf16[16,128,128]{2,1,0:T(8,128)(2,1)} %stack.2), calls=%async_computation | async-start | bytes 1048576 | tf_op jit(solution)/shard_map/all_to_all | solution.py:28
  17.3 2.1 all_gather.6
  21.4 0.9 broadcast_multiply_fusion.2
  22.4 1.0 fusion.22
  23.4 8.9 %all-to-all-done = bf16[16,128,128]{2,1,0:T(8,128)(2,1)S(1)} async-done(((bf16[16,128,128]{2,1,0:T(8,128)(2,1)}), bf16[16,128,128]{2,1,0:T(8,128)(2,1)S(1)}, u32[]{:S(2)}, u32[]{:S(2)}) %all-to-all-start) | async-done | bytes 524320 | tf_op jit(solution)/shard_map/all_to_all | solution.py:28
  32.3 3.0 %gather_fusion = bf16[128,128,128]{2,1,0:T(8,128)(2,1)} fusion(bf16[16,128,128]{2,1,0:T(8,128)(2,1)S(1)} %all-to-all-done, s32[1024]{0:T(1024)S(1)} %pad_clamp_fusion.1), kind=kCustom, calls=%fused_computation | custom fusion | bytes 8389120 | tf_op jit(solution)/shard_map/gather | solution.py:31
  35.3 11.0 %convolution_bitcast_fusion = f32[128,128,128]{1,2,0:T(8,128)} fusion(bf16[128,128,128]{2,1,0:T(8,128)(2,1)} %gather_fusion, s32[128,128,128]{2,1,0:T(8,128)} %param.9), kind=kOutput, calls=%fused_computation.3 | convolution fusion | flops 538968064 | bytes 20971520 | tf_op jit(solution)/shard_map/tij,tjf->tif/dot_general | solution.py:33
  46.3 9.3 %copy.29 = f32[128,128,128]{2,0,1:T(8,128)} copy(f32[128,128,128]{1,2,0:T(8,128)} %convolution_bitcast_fusion) | data formatting | bytes 16777216 | tf_op jit(solution)/shard_map/tij,tjf->tif/dot_general | solution.py:33
  55.6 6.2 %fusion.13 = f32[2,128,128]{2,0,1:T(2,128)S(1)} fusion(f32[128,128,128]{2,0,1:T(8,128)} %copy.29, s32[128]{0:T(128)S(1)} %copy-done.3), kind=kOutput, calls=%fused_computation.35 | convolution fusion | flops 50331904 | bytes 8520192 | tf_op jit(solution)/shard_map/tr,tif->rif/dot_general | solution.py:37
  62.5 1.9 all_gather.7
  64.4 14.4 %all-reduce.6.cloned.1.call-done = f32[256,128]{1,0:T(8,128)} async-done(((f32[256,128]{1,0:T(8,128)}), f32[256,128]{1,0:T(8,128)}) %all-reduce.6.cloned.1.call-update) | async-done | bytes 131088 | tf_op jit(solution)/shard_map/psum | solution.py:46
  78.9 0.9 multiply_convert_fusion.1
  80.1 0.9 fusion.3
  82.1 3.0 gather_fusion.1
  85.1 8.3 %convert_bitcast_fusion = bf16[128,128,128]{1,2,0:T(8,128)(2,1)} fusion(bf16[128,128,128]{2,1,0:T(8,128)(2,1)} %gather_fusion.1, s32[128,128,128]{2,1,0:T(8,128)} %param.9), kind=kOutput, calls=%fused_computation.2 | convolution fusion | flops 541065216 | bytes 16777216 | tf_op jit(solution)/shard_map/tij,tif->tjf/dot_general | solution.py:71
  93.4 6.7 %copy.32 = bf16[128,128,128]{2,0,1:T(8,128)(2,1)} copy(bf16[128,128,128]{1,2,0:T(8,128)(2,1)} %convert_bitcast_fusion) | data formatting | bytes 8388608 | tf_op jit(solution)/shard_map/convert_element_type | solution.py:73
  100.2 1.5 all-reduce.10.cloned.1.call-done
  101.8 2.9 fusion.10
  104.6 1.3 copy.33
  106.6 109.7 %all-reduce.8.cloned.1.call-done = (f32[128,256]{0,1:T(8,128)}, f32[128,256]{0,1:T(8,128)}) async-done(((f32[128,256]{0,1:T(8,128)}, f32[128,256]{0,1:T(8,128)}), (f32[128,256]{0,1:T(8,128)}, f32[128,256]{0,1:T(8,128)})) %all-reduce.8.cloned.1.call-update) | async-done | bytes 262160 | tf_op jit(solution)/shard_map/psum | solution.py:68
  216.3 1.0 broadcast_multiply_fusion
  218.9 77.1 %reduce-scatter.2.cloned.1.call-done = f32[128,128]{1,0:T(8,128)} async-done(((f32[2048,128]{1,0:T(8,128)}), f32[128,128]{1,0:T(8,128)}) %reduce-scatter.2.cloned.1.call-update) | async-done | bytes 65552 | tf_op jit(solution)/shard_map/reduce_scatter | solution.py:80
  296.0 1.6 convolution_add_fusion.1
  (30 shorter events, 6.5 us)
Async XLA Ops:
  7.2 72.6 %copy-start = (bf16[128,256]{1,0:T(8,128)(2,1)S(1)}, bf16[128,256]{1,0:T(8,128)(2,1)}, u32[]{:S(2)}) copy-start(bf16[128,256]{1,0:T(8,128)(2,1)} %param.15) | copy-start | bytes 196612
  8.9 23.4 %all-to-all-start = ((bf16[16,128,128]{2,1,0:T(8,128)(2,1)}), bf16[16,128,128]{2,1,0:T(8,128)(2,1)S(1)}, u32[]{:S(2)}, u32[]{:S(2)}) async-start(bf16[16,128,128]{2,1,0:T(8,128)(2,1)} %stack.2), calls=%async_computation | async-start | bytes 1048576 | tf_op jit(solution)/shard_map/all_to_all | solution.py:28
  17.2 61.6 %all-reduce.6.cloned.1.call-start = ((), (), s32[]{:S(2)}) async-start(), calls=%async_computation.2 | async-start | bytes 262144 | tf_op jit(solution)/shard_map/psum | solution.py:46
  46.3 9.3 %copy-start.3 = (s32[128]{0:T(128)S(1)}, s32[128]{0:T(128)}, u32[]{:S(2)}) copy-start(s32[128]{0:T(128)} %param.10) | copy-start | bytes 1540
  55.6 25.3 %copy-start.1 = (bf16[128,128]{1,0:T(8,128)(2,1)S(1)}, bf16[128,128]{1,0:T(8,128)(2,1)}, u32[]{:S(2)}) copy-start(bf16[128,128]{1,0:T(8,128)(2,1)} %param.8) | copy-start | bytes 98308
  62.5 39.2 %all-reduce.10.cloned.1.call-start = ((), (), s32[]{:S(2)}) async-start(), calls=%async_computation.5 | async-start | bytes 524288 | tf_op jit(solution)/shard_map/psum | solution.py:67
  82.0 134.3 %all-reduce.8.cloned.1.call-start = ((), (), s32[]{:S(2)}) async-start(), calls=%async_computation.4 | async-start | bytes 524288 | tf_op jit(solution)/shard_map/psum | solution.py:68
  101.7 194.3 %reduce-scatter.2.cloned.1.call-start = ((), (), s32[]{:S(2)}) async-start(), calls=%async_computation.3 | async-start | bytes 1114112 | tf_op jit(solution)/shard_map/reduce_scatter | solution.py:80
  101.7 194.3 %copy-start.2 = (bf16[128,256]{1,0:T(8,128)(2,1)S(1)}, bf16[128,256]{1,0:T(8,128)(2,1)}, u32[]{:S(2)}) copy-start(bf16[128,256]{1,0:T(8,128)(2,1)} %param.14) | copy-start | bytes 196612
Sparse Core Ops, SparseCore 0:
  62.6 16.2 all-reduce.5
  82.1 19.4 all-reduce.9
  107.0 109.3 all-reduce.7
  218.5 77.4 reduce-scatter.1
